TPU v7x, 32 devices: a whole 2x2x4 slice. The times are simulated.
32 devices in a mesh: gx: 2 (over x), gy: 4 (over z), gz: 4 (over y, core).
Axes of the slice: x: 2, y: 2, z: 4, core: 2. Of those that a mesh axis runs over, the one named last changes fastest.
Arguments:
- features: bfloat16 [2, 4, 4, 768, 256], P('gx', 'gy', 'gz'), may hold values from -6 to 6
- weight: bfloat16 [27, 256, 256], replicated, may hold values from -0.078125 to 0.078125
- upstream: bfloat16 [2, 4, 4, 768, 256], P('gx', 'gy', 'gz'), may hold values from -6 to 6
- send_rows: int32 [2, 4, 4, 6, 96], P('gx', 'gy', 'gz'), may hold values from 0 to 767
- in_rows: int32 [2, 4, 4, 27, 768], P('gx', 'gy', 'gz'), may hold values from 0 to 1343, as said below
- out_rows: int32 [2, 4, 4, 27, 768], P('gx', 'gy', 'gz'), may hold values from 0 to 767, each once within a row
- tap_pair_exists: int32 [2, 4, 4, 27, 768], P('gx', 'gy', 'gz'), may hold values from 0 to 1, as said below
Outputs:
- activated: bfloat16 [2, 4, 4, 768, 256], P('gx', 'gy', 'gz')
- grad_features: bfloat16 [2, 4, 4, 768, 256], P('gx', 'gy', 'gz')
- grad_weight: bfloat16 [27, 256, 256], replicated
Inputs may be any that keep to these rules, and one draw needn't show every extreme that they name: `in_rows`: rows below 768 are a device's own; row 768 + d * 96 + f is row f of face d of the extended rows. For each device and tap the 768 rows are distinct. `out_rows`: for each device and tap, every row appears exactly once. `tap_pair_exists`: the share of existing pairs differs from device to device and from tap to tap.
All inputs are finite; a program needn't handle non-finite values.
Results may differ from a plain program's by a relative error of at most 0.0053.
Values may be sent and summed in bfloat16 or wider, within the bound.
No kernel may reach another device: no remote copies, remote signals or barrier semaphores. Data moves between devices by JAX's collectives and lax.ppermute only.
A program may use at most 128 MiB of HBM per device.

v0:
```python
import jax
import jax.numpy as jnp
from jax import lax
from jax.sharding import PartitionSpec as P


def extended(cells, sides, width):
    for axis, dim in sides:
        count = lax.axis_size(axis)
        ends = count - 1
        head = lax.slice_in_dim(cells, 0, width, axis=dim)
        tail = lax.slice_in_dim(cells, cells.shape[dim] - width, cells.shape[dim], axis=dim)
        cells = jnp.concatenate(
            [
                lax.ppermute(tail, axis, [(i, (i + 1) % count) for i in range(ends)]),
                cells,
                lax.ppermute(head, axis, [((i + 1) % count, i) for i in range(ends)]),
            ],
            axis=dim,
        )
    return cells


def trade(stacked):
    along_x = extended(stacked[0:2], (("gx", 0),), 1)
    along_y = extended(stacked[2:4], (("gy", 0),), 1)
    along_z = extended(stacked[4:6], (("gz", 0),), 1)
    return jnp.stack([along_x[0], along_x[3], along_y[0], along_y[3], along_z[0], along_z[3]])


def pairing_tables(source_voxels, target_voxels, occupancy_flags, extended_rows):
    tap_count, own_rows = source_voxels.shape
    tap_index = jnp.arange(tap_count, dtype=jnp.int32)[:, None]
    pair_index = jnp.broadcast_to(
        jnp.arange(own_rows, dtype=jnp.int32)[None, :], (tap_count, own_rows)
    )
    inverse_out = (
        jnp.zeros((tap_count, own_rows), jnp.int32).at[tap_index, target_voxels].set(pair_index)
    )
    live_at_out = jnp.take_along_axis(occupancy_flags, inverse_out, axis=1)
    source_at_out = jnp.take_along_axis(source_voxels, inverse_out, axis=1)
    forward_source = jnp.where(live_at_out > 0, source_at_out, extended_rows)
    live_target = jnp.where(occupancy_flags > 0, target_voxels, own_rows)
    backward_target = (
        jnp.full((tap_count, extended_rows), own_rows, jnp.int32)
        .at[tap_index, source_voxels]
        .set(live_target)
    )
    return (forward_source, backward_target)


def convolution_forward_step(padded_zero, forward_source, weight, group_length):
    tap_count, own_rows = forward_source.shape
    channels = weight.shape[2]
    source_by_row = forward_source.T

    def advance(group_index, running):
        leading_tap = group_index * group_length
        picks = lax.dynamic_slice_in_dim(source_by_row, leading_tap, group_length, 1)
        kernels = lax.dynamic_slice_in_dim(weight, leading_tap, group_length, 0).reshape(
            group_length * channels, channels
        )

        def accumulate(current):
            gathered = padded_zero[picks].reshape(own_rows, group_length * channels)
            return current + jnp.dot(gathered, kernels, preferred_element_type=jnp.float32)

        return accumulate(running)

    start = jnp.zeros((own_rows, channels), jnp.float32)
    return lax.fori_loop(0, tap_count // group_length, advance, start)


def convolution_backward_step(
    padded_features, backward_target, weight, gradient_zero, group_length
):
    tap_count, extended_rows = backward_target.shape
    channels = weight.shape[2]
    target_by_row = backward_target.T
    flipped = jnp.transpose(weight, (0, 2, 1))

    def advance(group_index, carried):
        leading_tap = group_index * group_length
        places = lax.dynamic_slice_in_dim(target_by_row, leading_tap, group_length, 1)
        kernels = lax.dynamic_slice_in_dim(flipped, leading_tap, group_length, 0).reshape(
            group_length * channels, channels
        )

        def accumulate(current):
            grad_rows, grad_kernel = current
            chosen = gradient_zero[places].reshape(extended_rows, group_length * channels)
            grad_rows = grad_rows + jnp.dot(chosen, kernels, preferred_element_type=jnp.float32)
            kernel_term = lax.dot_general(
                padded_features,
                chosen,
                (((0,), (0,)), ((), ())),
                preferred_element_type=jnp.float32,
            )
            kernel_term = jnp.transpose(
                kernel_term.reshape(channels, group_length, channels), (1, 0, 2)
            )
            grad_kernel = lax.dynamic_update_slice_in_dim(grad_kernel, kernel_term, leading_tap, 0)
            return (grad_rows, grad_kernel)

        return accumulate(carried)

    start = (
        jnp.zeros((extended_rows, channels), jnp.float32),
        jnp.zeros((tap_count, channels, channels), jnp.float32),
    )
    return lax.fori_loop(0, tap_count // group_length, advance, start)


def shards(features, weight, upstream, send_rows, in_rows, out_rows, tap_pair_exists):
    own_features = features[0, 0, 0]
    own_rows, channels = own_features.shape
    sends = send_rows[0, 0, 0]
    face_rows = sends.shape[1]
    source_voxels = in_rows[0, 0, 0]
    target_voxels = out_rows[0, 0, 0]
    occupancy_flags = tap_pair_exists[0, 0, 0]
    sent = own_features[sends]
    incoming = trade(sent)
    padded_features = jnp.concatenate(
        [own_features, incoming.reshape(6 * face_rows, channels)], axis=0
    )
    extended_rows = padded_features.shape[0]
    padded_zero = jnp.concatenate([padded_features, jnp.zeros((1, channels), jnp.bfloat16)], axis=0)
    forward_source, backward_target = pairing_tables(
        source_voxels, target_voxels, occupancy_flags, extended_rows
    )
    group_length, skip_dead = (9, False)
    linear_response = convolution_forward_step(padded_zero, forward_source, weight, group_length)
    sigmoid = jax.nn.sigmoid(linear_response)
    activated = (linear_response * sigmoid).astype(jnp.bfloat16)
    derivative = sigmoid * (1.0 + linear_response * (1.0 - sigmoid))
    preactivation_gradient = (upstream[0, 0, 0].astype(jnp.float32) * derivative).astype(
        jnp.bfloat16
    )
    gradient_zero = jnp.concatenate(
        [preactivation_gradient, jnp.zeros((1, channels), jnp.bfloat16)], axis=0
    )
    grad_extended, weight_partial = convolution_backward_step(
        padded_features, backward_target, weight, gradient_zero, group_length
    )
    devices_all = lax.axis_size("gx") * lax.axis_size("gy") * lax.axis_size("gz")
    scaling = float(devices_all * own_rows) ** (-0.5)
    summed = lax.psum(weight_partial, ("gx", "gy", "gz"))
    grad_weight = (summed * scaling).astype(jnp.bfloat16)
    faces_back = grad_extended[own_rows:].astype(jnp.bfloat16).reshape(6, face_rows, channels)
    returned = trade(faces_back)
    grad_features = (
        grad_extended[:own_rows]
        .at[sends.reshape(-1)]
        .add(returned.reshape(-1, channels).astype(jnp.float32))
    )
    activated = activated[None, None, None]
    grad_features = grad_features.astype(jnp.bfloat16)[None, None, None]
    return (activated, grad_features, grad_weight)


def solution(mesh):
    return jax.shard_map(
        shards,
        mesh=mesh,
        in_specs=(
            P("gx", "gy", "gz", None, None),
            P(),
            P("gx", "gy", "gz", None, None),
            P("gx", "gy", "gz", None, None),
            P("gx", "gy", "gz", None, None),
            P("gx", "gy", "gz", None, None),
            P("gx", "gy", "gz", None, None),
        ),
        out_specs=(P("gx", "gy", "gz", None, None), P("gx", "gy", "gz", None, None), P()),
        check_vma=False,
    )
```

profile of v0, /device:TPU:0, one launch (start us, length us, event | category | flops | bytes accessed | tf_op | source)
XLA Modules:
  0.0 1032.5 jit_solution(6745703560755910110)
XLA Ops:
  16.9 5.6 collective-permute-start.2
  32.9 76.2 %scatter_custom_fusion.1 = s32[20736]{0:T(1024)S(1)} fusion(s32[20736]{0:T(1024)S(1)} %reshape.225, s32[20736]{0:T(1024)S(1)} %reshape.227, s32[]{:T(128)} %constant.100.clone.1), kind=kCustom, calls=%fused_computation.70 | custom fusion | bytes 82948
  109.2 156.1 %gather_fusion.4 = s32[20736]{0:T(1024)S(1)} fusion(s32[27,768]{1,0:T(8,128)S(1)} %bitcast.88, s32[20736]{0:T(1024)S(1)} %reshape.270), kind=kCustom, calls=%fused_computation.3.clone | custom fusion | bytes 331776 | tf_op jit(solution)/shard_map/jit(take_along_axis)/gather | solution.py:41
  265.4 156.1 %gather_fusion.3 = s32[20736]{0:T(1024)S(1)} fusion(s32[27,768]{1,0:T(8,128)S(1)} %bitcast.89, s32[20736]{0:T(1024)S(1)} %reshape.270), kind=kCustom, calls=%fused_computation.clone | custom fusion | bytes 331776 | tf_op jit(solution)/shard_map/jit(take_along_axis)/gather | solution.py:40
  421.7 76.3 %scatter_custom_fusion.2 = s32[36288]{0:T(1024)S(1)} fusion(s32[20736]{0:T(1024)S(1)} %reshape.231, s32[20736]{0:T(1024)S(1)} %reshape.233, s32[]{:T(128)} %constant.102.clone.1), kind=kCustom, calls=%fused_computation.54 | custom fusion | bytes 145156
  498.1 5.7 copy.22
  511.2 100.8 %while.30 = (s32[]{:T(128)}, f32[768,256]{1,0:T(8,128)S(1)}, s32[768,27]{0,1:T(8,128)S(1)}, bf16[1345,256]{1,0:T(8,128)(2,1)S(1)}, bf16[27,256,256]{2,1,0:T(8,12...) while((s32[]{:T(128)}, f32[768,256]{1,0:T(8,128)S(1)}, s32[768,27]{0,1:T(8,128)S(1)}, ...), condition=%wide.region_2.4_spmd.clone, body=%wide.region_1.3_spmd.clone.sunk | while | flops 906390784 | bytes 23505060 | solution.py:71
  511.8 20.0 %gather_fusion = bf16[6912,256]{1,0:T(8,128)(2,1)} fusion(bf16[1345,256]{1,0:T(8,128)(2,1)S(1)} %get-tuple-element.424, s32[7168]{0:T(1024)S(1)} %pad_clamp_fusion.5), kind=kCustom, calls=%fused_computation.1.clone.clone.1 | custom fusion | bytes 7105536 | tf_op jit(solution)/shard_map/while/body/eval_jaxpr/gather | solution.py:65
  531.7 7.8 reshape.303
  545.3 20.0 %gather_fusion = bf16[6912,256]{1,0:T(8,128)(2,1)} fusion(bf16[1345,256]{1,0:T(8,128)(2,1)S(1)} %get-tuple-element.424, s32[7168]{0:T(1024)S(1)} %pad_clamp_fusion.5), kind=kCustom, calls=%fused_computation.1.clone.clone.1 | custom fusion | bytes 7105536 | tf_op jit(solution)/shard_map/while/body/eval_jaxpr/gather | solution.py:65
  565.3 7.8 reshape.303
  578.9 20.0 %gather_fusion = bf16[6912,256]{1,0:T(8,128)(2,1)} fusion(bf16[1345,256]{1,0:T(8,128)(2,1)S(1)} %get-tuple-element.424, s32[7168]{0:T(1024)S(1)} %pad_clamp_fusion.5), kind=kCustom, calls=%fused_computation.1.clone.clone.1 | custom fusion | bytes 7105536 | tf_op jit(solution)/shard_map/while/body/eval_jaxpr/gather | solution.py:65
  598.9 7.8 reshape.303
  616.8 238.7 %while.31 = (s32[]{:T(128)}, f32[1344,256]{1,0:T(8,128)}, f32[27,256,256]{2,1,0:T(8,128)}, s32[1344,27]{0,1:T(8,128)S(1)}, bf16[769,256]{1,0:T(8,128)(2,1)S(1)},...) while((s32[]{:T(128)}, f32[1344,256]{1,0:T(8,128)}, ...), condition=%wide.region_5.7_spmd.clone, body=%wide.region_4.6_spmd.clone.sunk | while | flops 3171630592 | bytes 85074704 | solution.py:111
  617.6 34.7 %gather_fusion.1 = bf16[12096,256]{1,0:T(8,128)(2,1)} fusion(bf16[769,256]{1,0:T(8,128)(2,1)S(1)} %get-tuple-element.456, s32[12288]{0:T(1024)S(1)} %pad_clamp_fusion.6), kind=kCustom, calls=%fused_computation.2.clone.clone.1 | custom fusion | bytes 12434688 | tf_op jit(solution)/shard_map/while/body/eval_jaxpr/gather | solution.py:91
  652.3 11.9 %reshape.308 = bf16[1344,2304]{1,0:T(8,128)(2,1)} reshape(bf16[12096,256]{1,0:T(8,128)(2,1)} %gather_fusion.1) | data formatting | bytes 12386304 | tf_op jit(solution)/shard_map/while/body/eval_jaxpr/reshape | solution.py:91
  664.2 6.2 fusion.51
  674.2 12.8 %reshape.307 = bf16[1344,9,256]{2,1,0:T(8,128)(2,1)} reshape(bf16[12096,256]{1,0:T(8,128)(2,1)} %gather_fusion.1) | data formatting | bytes 12386304 | tf_op jit(solution)/shard_map/while/body/eval_jaxpr/gather | solution.py:91
  686.9 8.3 fusion.50
  697.2 34.7 %gather_fusion.1 = bf16[12096,256]{1,0:T(8,128)(2,1)} fusion(bf16[769,256]{1,0:T(8,128)(2,1)S(1)} %get-tuple-element.456, s32[12288]{0:T(1024)S(1)} %pad_clamp_fusion.6), kind=kCustom, calls=%fused_computation.2.clone.clone.1 | custom fusion | bytes 12434688 | tf_op jit(solution)/shard_map/while/body/eval_jaxpr/gather | solution.py:91
  731.9 11.9 %reshape.308 = bf16[1344,2304]{1,0:T(8,128)(2,1)} reshape(bf16[12096,256]{1,0:T(8,128)(2,1)} %gather_fusion.1) | data formatting | bytes 12386304 | tf_op jit(solution)/shard_map/while/body/eval_jaxpr/reshape | solution.py:91
  743.8 6.2 fusion.51
  753.7 12.8 %reshape.307 = bf16[1344,9,256]{2,1,0:T(8,128)(2,1)} reshape(bf16[12096,256]{1,0:T(8,128)(2,1)} %gather_fusion.1) | data formatting | bytes 12386304 | tf_op jit(solution)/shard_map/while/body/eval_jaxpr/gather | solution.py:91
  766.4 8.3 fusion.50
  776.7 34.7 %gather_fusion.1 = bf16[12096,256]{1,0:T(8,128)(2,1)} fusion(bf16[769,256]{1,0:T(8,128)(2,1)S(1)} %get-tuple-element.456, s32[12288]{0:T(1024)S(1)} %pad_clamp_fusion.6), kind=kCustom, calls=%fused_computation.2.clone.clone.1 | custom fusion | bytes 12434688 | tf_op jit(solution)/shard_map/while/body/eval_jaxpr/gather | solution.py:91
  811.4 11.9 %reshape.308 = bf16[1344,2304]{1,0:T(8,128)(2,1)} reshape(bf16[12096,256]{1,0:T(8,128)(2,1)} %gather_fusion.1) | data formatting | bytes 12386304 | tf_op jit(solution)/shard_map/while/body/eval_jaxpr/reshape | solution.py:91
  823.4 6.2 fusion.51
  833.2 12.8 %reshape.307 = bf16[1344,9,256]{2,1,0:T(8,128)(2,1)} reshape(bf16[12096,256]{1,0:T(8,128)(2,1)} %gather_fusion.1) | data formatting | bytes 12386304 | tf_op jit(solution)/shard_map/while/body/eval_jaxpr/gather | solution.py:91
  845.9 8.3 fusion.50
  875.0 6.7 scatter_custom_fusion
  882.5 137.4 %all-reduce.3.cloned.1.call-done = f32[27,256,256]{2,1,0:T(8,128)} async-done(((f32[27,256,256]{2,1,0:T(8,128)}), f32[27,256,256]{2,1,0:T(8,128)}) %all-reduce.3.cloned.1.call-update) | async-done | bytes 7077904 | tf_op jit(solution)/shard_map/psum | solution.py:148
  1019.9 5.7 multiply_convert_fusion
  (147 shorter events, 86.8 us)
Async XLA Ops:
  7.2 1012.7 %all-reduce.3.cloned.1.call-start = ((), (), s32[]{:S(2)}) async-start(), calls=%async_computation | async-start | bytes 14155776 | tf_op jit(solution)/shard_map/psum | solution.py:148
  11.2 498.7 %collective-permute-start.5 = (bf16[1,96,256]{2,1,0:T(8,128)(2,1)S(1)}, bf16[1,96,256]{2,1,0:T(8,128)(2,1)S(1)}, u32[]{:S(2)}, u32[]{:S(2)}) collective-permute-start(bf16[1,96,256]{2,1,0:T(8,128)(2,1)S(1)} %get-tuple-element.321), channel_id=1, source_target_pairs={{1,0},{2,1},{3,2},{5,4},{6,5},{7,6},{9,8},{10,9},{11,10},{13,12},{... | collective-permute-start | bytes 147464 | tf_op jit(solution)/shard_map/ppermute | solution.py:17
  12.5 497.3 %collective-permute-start.4 = (bf16[1,96,256]{2,1,0:T(8,128)(2,1)S(1)}, bf16[1,96,256]{2,1,0:T(8,128)(2,1)S(1)}, u32[]{:S(2)}, u32[]{:S(2)}) collective-permute-start(bf16[1,96,256]{2,1,0:T(8,128)(2,1)S(1)} %get-tuple-element.322), channel_id=1, source_target_pairs={{0,1},{1,2},{2,3},{4,5},{5,6},{6,7},{8,9},{9,10},{10,11},{12,13},{... | collective-permute-start | bytes 147464 | tf_op jit(solution)/shard_map/ppermute | solution.py:15
  15.6 494.3 %collective-permute-start.3 = (bf16[1,96,256]{2,1,0:T(8,128)(2,1)S(1)}, bf16[1,96,256]{2,1,0:T(8,128)(2,1)S(1)}, u32[]{:S(2)}, u32[]{:S(2)}) collective-permute-start(bf16[1,96,256]{2,1,0:T(8,128)(2,1)S(1)} %get-tuple-element.323), channel_id=1, source_target_pairs={{4,0},{8,4},{12,8},{5,1},{9,5},{13,9},{6,2},{10,6},{14,10},{7,3},{... | collective-permute-start | bytes 147464 | tf_op jit(solution)/shard_map/ppermute | solution.py:17
  16.9 493.0 %collective-permute-start.2 = (bf16[1,96,256]{2,1,0:T(8,128)(2,1)S(1)}, bf16[1,96,256]{2,1,0:T(8,128)(2,1)S(1)}, u32[]{:S(2)}, u32[]{:S(2)}) collective-permute-start(bf16[1,96,256]{2,1,0:T(8,128)(2,1)S(1)} %get-tuple-element.324), channel_id=1, source_target_pairs={{0,4},{4,8},{8,12},{1,5},{5,9},{9,13},{2,6},{6,10},{10,14},{3,7},{... | collective-permute-start | bytes 147464 | tf_op jit(solution)/shard_map/ppermute | solution.py:15
  22.5 481.4 %collective-permute-start = (bf16[1,96,256]{2,1,0:T(8,128)(2,1)S(1)}, bf16[1,96,256]{2,1,0:T(8,128)(2,1)S(1)}, u32[]{:S(2)}, u32[]{:S(2)}) collective-permute-start(bf16[1,96,256]{2,1,0:T(8,128)(2,1)S(1)} %get-tuple-element.326), channel_id=1, source_target_pairs={{0,16},{1,17},{2,18},{3,19},{4,20},{5,21},{6,22},{7,23},{8,24},{9,... | collective-permute-start | bytes 147464 | tf_op jit(solution)/shard_map/ppermute | solution.py:15
  265.3 156.2 %copy-start.6 = (s32[1,1,1,27,768]{4,2,3,1,0:T(1,128)S(1)}, s32[1,1,1,27,768]{4,2,3,1,0:T(1,128)}, u32[]{:S(2)}) copy-start(s32[1,1,1,27,768]{4,2,3,1,0:T(1,128)} %param.18) | copy-start | bytes 248836
  265.4 156.2 %copy-start.7 = (s32[1,1,1,27,768]{4,2,3,1,0:T(1,128)S(1)}, s32[1,1,1,27,768]{4,2,3,1,0:T(1,128)}, u32[]{:S(2)}) copy-start(s32[1,1,1,27,768]{4,2,3,1,0:T(1,128)} %param.19) | copy-start | bytes 248836
  421.5 88.4 %copy-start = (bf16[1,1,1,768,256]{4,3,2,1,0:T(8,128)(2,1)S(1)}, bf16[1,1,1,768,256]{4,3,2,1,0:T(8,128)(2,1)}, u32[]{:S(2)}) copy-start(bf16[1,1,1,768,256]{4,3,2,1,0:T(8,128)(2,1)} %param.13) | copy-start | bytes 1179652
  503.9 6.0 collective-permute-start.1
  511.2 100.8 %copy-start.5 = (bf16[1,1,1,768,256]{4,3,2,1,0:T(8,128)(2,1)S(1)}, bf16[1,1,1,768,256]{4,3,2,1,0:T(8,128)(2,1)}, u32[]{:S(2)}) copy-start(bf16[1,1,1,768,256]{4,3,2,1,0:T(8,128)(2,1)} %param.15) | copy-start | bytes 1179652
  652.3 11.9 %copy-start.4 = (bf16[1344,256]{1,0:T(8,128)(2,1)S(1)}, bf16[1344,256]{1,0:T(8,128)(2,1)}, u32[]{:S(2)}) copy-start(bf16[1344,256]{1,0:T(8,128)(2,1)} %get-tuple-element.458) | copy-start | bytes 2064388 | tf_op jit(solution)/shard_map/while
  674.1 12.8 %copy-start.1 = (f32[1344,256]{1,0:T(8,128)S(1)}, f32[1344,256]{1,0:T(8,128)}, u32[]{:S(2)}) copy-start(f32[1344,256]{1,0:T(8,128)} %get-tuple-element.442) | copy-start | bytes 4128772 | tf_op jit(solution)/shard_map/while
  695.2 1.2 copy-start.2
  731.9 11.9 %copy-start.4 = (bf16[1344,256]{1,0:T(8,128)(2,1)S(1)}, bf16[1344,256]{1,0:T(8,128)(2,1)}, u32[]{:S(2)}) copy-start(bf16[1344,256]{1,0:T(8,128)(2,1)} %get-tuple-element.458) | copy-start | bytes 2064388 | tf_op jit(solution)/shard_map/while
  753.7 12.8 %copy-start.1 = (f32[1344,256]{1,0:T(8,128)S(1)}, f32[1344,256]{1,0:T(8,128)}, u32[]{:S(2)}) copy-start(f32[1344,256]{1,0:T(8,128)} %get-tuple-element.442) | copy-start | bytes 4128772 | tf_op jit(solution)/shard_map/while
  774.7 1.2 copy-start.2
  811.4 11.9 %copy-start.4 = (bf16[1344,256]{1,0:T(8,128)(2,1)S(1)}, bf16[1344,256]{1,0:T(8,128)(2,1)}, u32[]{:S(2)}) copy-start(bf16[1344,256]{1,0:T(8,128)(2,1)} %get-tuple-element.458) | copy-start | bytes 2064388 | tf_op jit(solution)/shard_map/while
  833.2 12.8 %copy-start.1 = (f32[1344,256]{1,0:T(8,128)S(1)}, f32[1344,256]{1,0:T(8,128)}, u32[]{:S(2)}) copy-start(f32[1344,256]{1,0:T(8,128)} %get-tuple-element.442) | copy-start | bytes 4128772 | tf_op jit(solution)/shard_map/while
  854.2 1.2 copy-start.2
  855.4 0.7 copy-start.8
  855.4 1.4 copy-start.3
  856.9 11.9 %collective-permute-start.6 = (bf16[1,96,256]{2,1,0:T(8,128)(2,1)S(1)}, bf16[1,96,256]{2,1,0:T(8,128)(2,1)S(1)}, u32[]{:S(2)}, u32[]{:S(2)}) collective-permute-start(bf16[1,96,256]{2,1,0:T(8,128)(2,1)S(1)} %get-tuple-element.320), channel_id=1, source_target_pairs={{0,16},{1,17},{2,18},{3,19},{4,20},{5,21},{6,22},{7,23},{8,24},{9,... | collective-permute-start | bytes 147464 | tf_op jit(solution)/shard_map/ppermute | solution.py:15
  858.6 16.4 %collective-permute-start.11 = (bf16[1,96,256]{2,1,0:T(8,128)(2,1)S(1)}, bf16[1,96,256]{2,1,0:T(8,128)(2,1)S(1)}, u32[]{:S(2)}, u32[]{:S(2)}) collective-permute-start(bf16[1,96,256]{2,1,0:T(8,128)(2,1)S(1)} %get-tuple-element.315), channel_id=1, source_target_pairs={{1,0},{2,1},{3,2},{5,4},{6,5},{7,6},{9,8},{10,9},{11,10},{13,12},{... | collective-permute-start | bytes 147464 | tf_op jit(solution)/shard_map/ppermute | solution.py:17
  859.9 15.1 %collective-permute-start.10 = (bf16[1,96,256]{2,1,0:T(8,128)(2,1)S(1)}, bf16[1,96,256]{2,1,0:T(8,128)(2,1)S(1)}, u32[]{:S(2)}, u32[]{:S(2)}) collective-permute-start(bf16[1,96,256]{2,1,0:T(8,128)(2,1)S(1)} %get-tuple-element.316), channel_id=1, source_target_pairs={{0,1},{1,2},{2,3},{4,5},{5,6},{6,7},{8,9},{9,10},{10,11},{12,13},{... | collective-permute-start | bytes 147464 | tf_op jit(solution)/shard_map/ppermute | solution.py:15
  862.9 12.0 %collective-permute-start.9 = (bf16[1,96,256]{2,1,0:T(8,128)(2,1)S(1)}, bf16[1,96,256]{2,1,0:T(8,128)(2,1)S(1)}, u32[]{:S(2)}, u32[]{:S(2)}) collective-permute-start(bf16[1,96,256]{2,1,0:T(8,128)(2,1)S(1)} %get-tuple-element.317), channel_id=1, source_target_pairs={{4,0},{8,4},{12,8},{5,1},{9,5},{13,9},{6,2},{10,6},{14,10},{7,3},{... | collective-permute-start | bytes 147464 | tf_op jit(solution)/shard_map/ppermute | solution.py:17
  864.2 10.7 %collective-permute-start.8 = (bf16[1,96,256]{2,1,0:T(8,128)(2,1)S(1)}, bf16[1,96,256]{2,1,0:T(8,128)(2,1)S(1)}, u32[]{:S(2)}, u32[]{:S(2)}) collective-permute-start(bf16[1,96,256]{2,1,0:T(8,128)(2,1)S(1)} %get-tuple-element.318), channel_id=1, source_target_pairs={{0,4},{4,8},{8,12},{1,5},{5,9},{9,13},{2,6},{6,10},{10,14},{3,7},{... | collective-permute-start | bytes 147464 | tf_op jit(solution)/shard_map/ppermute | solution.py:15
  868.8 6.1 collective-permute-start.7
Sparse Core Ops, SparseCore 0:
  855.6 164.2 all-reduce.2
where the time goes:
time: 1040 us; the launch traced here: 1030 us
  local copies, waits for them, and re-layouts  760 us (73%)
  waiting for transfers between devices  147 us (14%)
  matrix products  59.3 us (6%)
  starting transfers between devices  29.4 us (3%)
  other arithmetic  21.6 us (2%)
  between operations  14.6 us (1%)
    unnamed x29, local copies, waits for them, and re-layouts  161 us
    gather x3, local copies, waits for them, and re-layouts, pairing_tables(): live_at_out = jnp.take_along_axis(occupancy_flags, inverse_out, axis=1)  156 us
    gather x2, local copies, waits for them, and re-layouts, pairing_tables(): source_at_out = jnp.take_along_axis(source_voxels, inverse_out, axis=1)  156 us
    gather x6, local copies, waits for them, and re-layouts, accumulate(): gradient_zero[places].reshape(extended_rows, group_length * channels)  142 us
    psum x1, waiting for transfers between devices, shards(): summed = lax.psum(weight_partial, ('gx', 'gy', 'gz'))  137 us
    gather x6, local copies, waits for them, and re-layouts, accumulate(): gathered = padded_zero[picks].reshape(own_rows, group_length * channels)  83.2 us
    reshape x3, local copies, waits for them, and re-layouts, accumulate(): gradient_zero[places].reshape(extended_rows, group_length * channels)  35.8 us
    dot_general x3, matrix products, accumulate(): jnp.dot(chosen, kernels, preferred_element_type=jnp.float32)  24.9 us
  transfers between devices with their start and end apart: 13, of which 3 were waited for; matrix products, arithmetic and copies ran while one was open for 47% of the time, Pallas kernels for 0%

commit v1 on v0

--- a/solution.py
+++ b/solution.py
@@ -2,6 +2,7 @@
 import jax.numpy as jnp
 from jax import lax
 from jax.sharding import PartitionSpec as P
+from jax.lax import psum
 
 
 def extended(cells, sides, width):
@@ -145,7 +146,7 @@
     )
     devices_all = lax.axis_size("gx") * lax.axis_size("gy") * lax.axis_size("gz")
     scaling = float(devices_all * own_rows) ** (-0.5)
-    summed = lax.psum(weight_partial, ("gx", "gy", "gz"))
+    summed = psum(psum(weight_partial, ("gy", "gz")), "gx")
     grad_weight = (summed * scaling).astype(jnp.bfloat16)
     faces_back = grad_extended[own_rows:].astype(jnp.bfloat16).reshape(6, face_rows, channels)
     returned = trade(faces_back)

time: 1040 us -> 1190 us (1.14)
  waiting for transfers between devices: 147 us -> 305 us
    psum x1 -> x2, waiting for transfers between devices: 137 us -> 295 us  [shards(): summed = psum(psum(weight_partial, ('gy', 'gz')), 'gx')]
  transfers between devices with their start and end apart: 13 -> 14, of which waited for: 3 -> 4; matrix products, arithmetic and copies ran while one was open for 47% -> 41% of each run, Pallas kernels for 0% -> 0%
where the time goes in v1:
time: 1190 us
  local copies, waits for them, and re-layouts  759 us (64%)
  waiting for transfers between devices  305 us (26%)
  matrix products  59.3 us (5%)
  starting transfers between devices  31.2 us (3%)
  other arithmetic  21.6 us (2%)
  between operations  14.6 us (1%)
    psum x2, waiting for transfers between devices, shards(): summed = psum(psum(weight_partial, ('gy', 'gz')), 'gx')  295 us
    unnamed x29, local copies, waits for them, and re-layouts  160 us
    gather x3, local copies, waits for them, and re-layouts, pairing_tables(): live_at_out = jnp.take_along_axis(occupancy_flags, inverse_out, axis=1)  156 us
    gather x2, local copies, waits for them, and re-layouts, pairing_tables(): source_at_out = jnp.take_along_axis(source_voxels, inverse_out, axis=1)  156 us
    gather x6, local copies, waits for them, and re-layouts, accumulate(): gradient_zero[places].reshape(extended_rows, group_length * channels)  142 us
    gather x6, local copies, waits for them, and re-layouts, accumulate(): gathered = padded_zero[picks].reshape(own_rows, group_length * channels)  83.2 us
    reshape x3, local copies, waits for them, and re-layouts, accumulate(): gradient_zero[places].reshape(extended_rows, group_length * channels)  35.8 us
    dot_general x3, matrix products, accumulate(): jnp.dot(chosen, kernels, preferred_element_type=jnp.float32)  24.9 us
  transfers between devices with their start and end apart: 14, of which 4 were waited for; matrix products, arithmetic and copies ran while one was open for 41% of the time, Pallas kernels for 0%

profile of v1, /device:TPU:0, one launch (start us, length us, event | category | flops | bytes accessed | tf_op | source)
XLA Modules:
  0.0 1191.6 jit_solution(16034327733969883778)
XLA Ops:
  32.9 76.2 %scatter_custom_fusion.1 = s32[20736]{0:T(1024)S(1)} fusion(s32[20736]{0:T(1024)S(1)} %reshape.225, s32[20736]{0:T(1024)S(1)} %reshape.227, s32[]{:T(128)} %constant.100.clone.1), kind=kCustom, calls=%fused_computation.70 | custom fusion | bytes 82948
  109.2 156.1 %gather_fusion.4 = s32[20736]{0:T(1024)S(1)} fusion(s32[27,768]{1,0:T(8,128)S(1)} %bitcast.88, s32[20736]{0:T(1024)S(1)} %reshape.270), kind=kCustom, calls=%fused_computation.3.clone | custom fusion | bytes 331776 | tf_op jit(solution)/shard_map/jit(take_along_axis)/gather | solution.py:42
  265.4 156.1 %gather_fusion.3 = s32[20736]{0:T(1024)S(1)} fusion(s32[27,768]{1,0:T(8,128)S(1)} %bitcast.89, s32[20736]{0:T(1024)S(1)} %reshape.270), kind=kCustom, calls=%fused_computation.clone | custom fusion | bytes 331776 | tf_op jit(solution)/shard_map/jit(take_along_axis)/gather | solution.py:41
  421.7 76.3 %scatter_custom_fusion.2 = s32[36288]{0:T(1024)S(1)} fusion(s32[20736]{0:T(1024)S(1)} %reshape.231, s32[20736]{0:T(1024)S(1)} %reshape.233, s32[]{:T(128)} %constant.102.clone.1), kind=kCustom, calls=%fused_computation.54 | custom fusion | bytes 145156
  511.2 100.8 %while.30 = (s32[]{:T(128)}, f32[768,256]{1,0:T(8,128)S(1)}, s32[768,27]{0,1:T(8,128)S(1)}, bf16[1345,256]{1,0:T(8,128)(2,1)S(1)}, bf16[27,256,256]{2,1,0:T(8,12...) while((s32[]{:T(128)}, f32[768,256]{1,0:T(8,128)S(1)}, s32[768,27]{0,1:T(8,128)S(1)}, ...), condition=%wide.region_2.4_spmd.clone, body=%wide.region_1.3_spmd.clone.sunk | while | flops 906390784 | bytes 23505060 | solution.py:72
  511.8 20.0 %gather_fusion = bf16[6912,256]{1,0:T(8,128)(2,1)} fusion(bf16[1345,256]{1,0:T(8,128)(2,1)S(1)} %get-tuple-element.424, s32[7168]{0:T(1024)S(1)} %pad_clamp_fusion.5), kind=kCustom, calls=%fused_computation.1.clone.clone.1 | custom fusion | bytes 7105536 | tf_op jit(solution)/shard_map/while/body/eval_jaxpr/gather | solution.py:66
  531.7 7.8 reshape.303
  545.3 20.0 %gather_fusion = bf16[6912,256]{1,0:T(8,128)(2,1)} fusion(bf16[1345,256]{1,0:T(8,128)(2,1)S(1)} %get-tuple-element.424, s32[7168]{0:T(1024)S(1)} %pad_clamp_fusion.5), kind=kCustom, calls=%fused_computation.1.clone.clone.1 | custom fusion | bytes 7105536 | tf_op jit(solution)/shard_map/while/body/eval_jaxpr/gather | solution.py:66
  565.3 7.8 reshape.303
  578.9 20.0 %gather_fusion = bf16[6912,256]{1,0:T(8,128)(2,1)} fusion(bf16[1345,256]{1,0:T(8,128)(2,1)S(1)} %get-tuple-element.424, s32[7168]{0:T(1024)S(1)} %pad_clamp_fusion.5), kind=kCustom, calls=%fused_computation.1.clone.clone.1 | custom fusion | bytes 7105536 | tf_op jit(solution)/shard_map/while/body/eval_jaxpr/gather | solution.py:66
  598.9 7.8 reshape.303
  616.8 238.7 %while.31 = (s32[]{:T(128)}, f32[1344,256]{1,0:T(8,128)}, f32[27,256,256]{2,1,0:T(8,128)}, s32[1344,27]{0,1:T(8,128)S(1)}, bf16[769,256]{1,0:T(8,128)(2,1)S(1)},...) while((s32[]{:T(128)}, f32[1344,256]{1,0:T(8,128)}, ...), condition=%wide.region_5.7_spmd.clone, body=%wide.region_4.6_spmd.clone.sunk | while | flops 3171630592 | bytes 85074704 | solution.py:112
  617.6 34.7 %gather_fusion.1 = bf16[12096,256]{1,0:T(8,128)(2,1)} fusion(bf16[769,256]{1,0:T(8,128)(2,1)S(1)} %get-tuple-element.456, s32[12288]{0:T(1024)S(1)} %pad_clamp_fusion.6), kind=kCustom, calls=%fused_computation.2.clone.clone.1 | custom fusion | bytes 12434688 | tf_op jit(solution)/shard_map/while/body/eval_jaxpr/gather | solution.py:92
  652.3 11.9 %reshape.308 = bf16[1344,2304]{1,0:T(8,128)(2,1)} reshape(bf16[12096,256]{1,0:T(8,128)(2,1)} %gather_fusion.1) | data formatting | bytes 12386304 | tf_op jit(solution)/shard_map/while/body/eval_jaxpr/reshape | solution.py:92
  664.2 6.2 fusion.51
  674.2 12.8 %reshape.307 = bf16[1344,9,256]{2,1,0:T(8,128)(2,1)} reshape(bf16[12096,256]{1,0:T(8,128)(2,1)} %gather_fusion.1) | data formatting | bytes 12386304 | tf_op jit(solution)/shard_map/while/body/eval_jaxpr/gather | solution.py:92
  686.9 8.3 fusion.50
  697.2 34.7 %gather_fusion.1 = bf16[12096,256]{1,0:T(8,128)(2,1)} fusion(bf16[769,256]{1,0:T(8,128)(2,1)S(1)} %get-tuple-element.456, s32[12288]{0:T(1024)S(1)} %pad_clamp_fusion.6), kind=kCustom, calls=%fused_computation.2.clone.clone.1 | custom fusion | bytes 12434688 | tf_op jit(solution)/shard_map/while/body/eval_jaxpr/gather | solution.py:92
  731.9 11.9 %reshape.308 = bf16[1344,2304]{1,0:T(8,128)(2,1)} reshape(bf16[12096,256]{1,0:T(8,128)(2,1)} %gather_fusion.1) | data formatting | bytes 12386304 | tf_op jit(solution)/shard_map/while/body/eval_jaxpr/reshape | solution.py:92
  743.8 6.2 fusion.51
  753.7 12.8 %reshape.307 = bf16[1344,9,256]{2,1,0:T(8,128)(2,1)} reshape(bf16[12096,256]{1,0:T(8,128)(2,1)} %gather_fusion.1) | data formatting | bytes 12386304 | tf_op jit(solution)/shard_map/while/body/eval_jaxpr/gather | solution.py:92
  766.4 8.3 fusion.50
  776.7 34.7 %gather_fusion.1 = bf16[12096,256]{1,0:T(8,128)(2,1)} fusion(bf16[769,256]{1,0:T(8,128)(2,1)S(1)} %get-tuple-element.456, s32[12288]{0:T(1024)S(1)} %pad_clamp_fusion.6), kind=kCustom, calls=%fused_computation.2.clone.clone.1 | custom fusion | bytes 12434688 | tf_op jit(solution)/shard_map/while/body/eval_jaxpr/gather | solution.py:92
  811.4 11.9 %reshape.308 = bf16[1344,2304]{1,0:T(8,128)(2,1)} reshape(bf16[12096,256]{1,0:T(8,128)(2,1)} %gather_fusion.1) | data formatting | bytes 12386304 | tf_op jit(solution)/shard_map/while/body/eval_jaxpr/reshape | solution.py:92
  823.4 6.2 fusion.51
  833.2 12.8 %reshape.307 = bf16[1344,9,256]{2,1,0:T(8,128)(2,1)} reshape(bf16[12096,256]{1,0:T(8,128)(2,1)} %gather_fusion.1) | data formatting | bytes 12386304 | tf_op jit(solution)/shard_map/while/body/eval_jaxpr/gather | solution.py:92
  845.9 8.3 fusion.50
  855.5 149.8 %all-reduce.4.cloned.1.call-done = f32[27,256,256]{2,1,0:T(8,128)} async-done(((f32[27,256,256]{2,1,0:T(8,128)}), f32[27,256,256]{2,1,0:T(8,128)}) %all-reduce.4.cloned.1.call-update) | async-done | bytes 7077904 | tf_op jit(solution)/shard_map/psum | solution.py:149
  1020.5 6.1 collective-permute-done.7
  1026.7 6.7 scatter_custom_fusion
  1034.2 144.8 %all-reduce.6.cloned.1.call-done = f32[27,256,256]{2,1,0:T(8,128)} async-done(((f32[27,256,256]{2,1,0:T(8,128)}), f32[27,256,256]{2,1,0:T(8,128)}) %all-reduce.6.cloned.1.call-update) | async-done | bytes 7077904 | tf_op jit(solution)/shard_map/psum | solution.py:149
  1179.1 5.7 multiply_convert_fusion
  (150 shorter events, 93.9 us)
Async XLA Ops:
  7.2 998.1 %all-reduce.4.cloned.1.call-start = ((), (), s32[]{:S(2)}) async-start(), calls=%async_computation | async-start | bytes 14155776 | tf_op jit(solution)/shard_map/psum | solution.py:149
  11.2 498.7 %collective-permute-start.5 = (bf16[1,96,256]{2,1,0:T(8,128)(2,1)S(1)}, bf16[1,96,256]{2,1,0:T(8,128)(2,1)S(1)}, u32[]{:S(2)}, u32[]{:S(2)}) collective-permute-start(bf16[1,96,256]{2,1,0:T(8,128)(2,1)S(1)} %get-tuple-element.321), channel_id=1, source_target_pairs={{1,0},{2,1},{3,2},{5,4},{6,5},{7,6},{9,8},{10,9},{11,10},{13,12},{... | collective-permute-start | bytes 147464 | tf_op jit(solution)/shard_map/ppermute | solution.py:18
  12.5 497.3 %collective-permute-start.4 = (bf16[1,96,256]{2,1,0:T(8,128)(2,1)S(1)}, bf16[1,96,256]{2,1,0:T(8,128)(2,1)S(1)}, u32[]{:S(2)}, u32[]{:S(2)}) collective-permute-start(bf16[1,96,256]{2,1,0:T(8,128)(2,1)S(1)} %get-tuple-element.322), channel_id=1, source_target_pairs={{0,1},{1,2},{2,3},{4,5},{5,6},{6,7},{8,9},{9,10},{10,11},{12,13},{... | collective-permute-start | bytes 147464 | tf_op jit(solution)/shard_map/ppermute | solution.py:16
  15.6 494.3 %collective-permute-start.3 = (bf16[1,96,256]{2,1,0:T(8,128)(2,1)S(1)}, bf16[1,96,256]{2,1,0:T(8,128)(2,1)S(1)}, u32[]{:S(2)}, u32[]{:S(2)}) collective-permute-start(bf16[1,96,256]{2,1,0:T(8,128)(2,1)S(1)} %get-tuple-element.323), channel_id=1, source_target_pairs={{4,0},{8,4},{12,8},{5,1},{9,5},{13,9},{6,2},{10,6},{14,10},{7,3},{... | collective-permute-start | bytes 147464 | tf_op jit(solution)/shard_map/ppermute | solution.py:18
  16.9 493.0 %collective-permute-start.2 = (bf16[1,96,256]{2,1,0:T(8,128)(2,1)S(1)}, bf16[1,96,256]{2,1,0:T(8,128)(2,1)S(1)}, u32[]{:S(2)}, u32[]{:S(2)}) collective-permute-start(bf16[1,96,256]{2,1,0:T(8,128)(2,1)S(1)} %get-tuple-element.324), channel_id=1, source_target_pairs={{0,4},{4,8},{8,12},{1,5},{5,9},{9,13},{2,6},{6,10},{10,14},{3,7},{... | collective-permute-start | bytes 147464 | tf_op jit(solution)/shard_map/ppermute | solution.py:16
  22.5 481.4 %collective-permute-start = (bf16[1,96,256]{2,1,0:T(8,128)(2,1)S(1)}, bf16[1,96,256]{2,1,0:T(8,128)(2,1)S(1)}, u32[]{:S(2)}, u32[]{:S(2)}) collective-permute-start(bf16[1,96,256]{2,1,0:T(8,128)(2,1)S(1)} %get-tuple-element.326), channel_id=1, source_target_pairs={{0,16},{1,17},{2,18},{3,19},{4,20},{5,21},{6,22},{7,23},{8,24},{9,... | collective-permute-start | bytes 147464 | tf_op jit(solution)/shard_map/ppermute | solution.py:16
  265.3 156.2 %copy-start.6 = (s32[1,1,1,27,768]{4,2,3,1,0:T(1,128)S(1)}, s32[1,1,1,27,768]{4,2,3,1,0:T(1,128)}, u32[]{:S(2)}) copy-start(s32[1,1,1,27,768]{4,2,3,1,0:T(1,128)} %param.18) | copy-start | bytes 248836
  265.4 156.2 %copy-start.7 = (s32[1,1,1,27,768]{4,2,3,1,0:T(1,128)S(1)}, s32[1,1,1,27,768]{4,2,3,1,0:T(1,128)}, u32[]{:S(2)}) copy-start(s32[1,1,1,27,768]{4,2,3,1,0:T(1,128)} %param.19) | copy-start | bytes 248836
  421.5 88.4 %copy-start = (bf16[1,1,1,768,256]{4,3,2,1,0:T(8,128)(2,1)S(1)}, bf16[1,1,1,768,256]{4,3,2,1,0:T(8,128)(2,1)}, u32[]{:S(2)}) copy-start(bf16[1,1,1,768,256]{4,3,2,1,0:T(8,128)(2,1)} %param.13) | copy-start | bytes 1179652
  503.9 6.0 collective-permute-start.1
  511.2 100.8 %copy-start.5 = (bf16[1,1,1,768,256]{4,3,2,1,0:T(8,128)(2,1)S(1)}, bf16[1,1,1,768,256]{4,3,2,1,0:T(8,128)(2,1)}, u32[]{:S(2)}) copy-start(bf16[1,1,1,768,256]{4,3,2,1,0:T(8,128)(2,1)} %param.15) | copy-start | bytes 1179652
  652.3 11.9 %copy-start.4 = (bf16[1344,256]{1,0:T(8,128)(2,1)S(1)}, bf16[1344,256]{1,0:T(8,128)(2,1)}, u32[]{:S(2)}) copy-start(bf16[1344,256]{1,0:T(8,128)(2,1)} %get-tuple-element.458) | copy-start | bytes 2064388 | tf_op jit(solution)/shard_map/while
  674.1 12.8 %copy-start.1 = (f32[1344,256]{1,0:T(8,128)S(1)}, f32[1344,256]{1,0:T(8,128)}, u32[]{:S(2)}) copy-start(f32[1344,256]{1,0:T(8,128)} %get-tuple-element.442) | copy-start | bytes 4128772 | tf_op jit(solution)/shard_map/while
  695.2 1.2 copy-start.2
  731.9 11.9 %copy-start.4 = (bf16[1344,256]{1,0:T(8,128)(2,1)S(1)}, bf16[1344,256]{1,0:T(8,128)(2,1)}, u32[]{:S(2)}) copy-start(bf16[1344,256]{1,0:T(8,128)(2,1)} %get-tuple-element.458) | copy-start | bytes 2064388 | tf_op jit(solution)/shard_map/while
  753.7 12.8 %copy-start.1 = (f32[1344,256]{1,0:T(8,128)S(1)}, f32[1344,256]{1,0:T(8,128)}, u32[]{:S(2)}) copy-start(f32[1344,256]{1,0:T(8,128)} %get-tuple-element.442) | copy-start | bytes 4128772 | tf_op jit(solution)/shard_map/while
  774.7 1.2 copy-start.2
  811.4 11.9 %copy-start.4 = (bf16[1344,256]{1,0:T(8,128)(2,1)S(1)}, bf16[1344,256]{1,0:T(8,128)(2,1)}, u32[]{:S(2)}) copy-start(bf16[1344,256]{1,0:T(8,128)(2,1)} %get-tuple-element.458) | copy-start | bytes 2064388 | tf_op jit(solution)/shard_map/while
  833.2 12.8 %copy-start.1 = (f32[1344,256]{1,0:T(8,128)S(1)}, f32[1344,256]{1,0:T(8,128)}, u32[]{:S(2)}) copy-start(f32[1344,256]{1,0:T(8,128)} %get-tuple-element.442) | copy-start | bytes 4128772 | tf_op jit(solution)/shard_map/while
  854.2 1.2 copy-start.2
  855.4 149.9 %copy-start.8 = (s32[1,1,1,6,96]{4,2,3,1,0:T(1,128)S(1)}, s32[1,1,1,6,96]{4,2,3,1,0:T(1,128)}, u32[]{:S(2)}) copy-start(s32[1,1,1,6,96]{4,2,3,1,0:T(1,128)} %param.16) | copy-start | bytes 6916
  855.4 150.0 %copy-start.3 = (f32[1344,256]{1,0:T(8,128)S(1)}, f32[1344,256]{1,0:T(8,128)}, u32[]{:S(2)}) copy-start(f32[1344,256]{1,0:T(8,128)} %get-tuple-element.224) | copy-start | bytes 4128772
  855.5 323.6 %all-reduce.6.cloned.1.call-start = ((), (), s32[]{:S(2)}) async-start(), calls=%async_computation.1 | async-start | bytes 14155776 | tf_op jit(solution)/shard_map/psum | solution.py:149
  1005.5 13.7 %collective-permute-start.6 = (bf16[1,96,256]{2,1,0:T(8,128)(2,1)S(1)}, bf16[1,96,256]{2,1,0:T(8,128)(2,1)S(1)}, u32[]{:S(2)}, u32[]{:S(2)}) collective-permute-start(bf16[1,96,256]{2,1,0:T(8,128)(2,1)S(1)} %get-tuple-element.320), channel_id=1, source_target_pairs={{0,16},{1,17},{2,18},{3,19},{4,20},{5,21},{6,22},{7,23},{8,24},{9,... | collective-permute-start | bytes 147464 | tf_op jit(solution)/shard_map/ppermute | solution.py:16
  1009.0 17.7 %collective-permute-start.11 = (bf16[1,96,256]{2,1,0:T(8,128)(2,1)S(1)}, bf16[1,96,256]{2,1,0:T(8,128)(2,1)S(1)}, u32[]{:S(2)}, u32[]{:S(2)}) collective-permute-start(bf16[1,96,256]{2,1,0:T(8,128)(2,1)S(1)} %get-tuple-element.315), channel_id=1, source_target_pairs={{1,0},{2,1},{3,2},{5,4},{6,5},{7,6},{9,8},{10,9},{11,10},{13,12},{... | collective-permute-start | bytes 147464 | tf_op jit(solution)/shard_map/ppermute | solution.py:18
  1010.3 16.3 %collective-permute-start.10 = (bf16[1,96,256]{2,1,0:T(8,128)(2,1)S(1)}, bf16[1,96,256]{2,1,0:T(8,128)(2,1)S(1)}, u32[]{:S(2)}, u32[]{:S(2)}) collective-permute-start(bf16[1,96,256]{2,1,0:T(8,128)(2,1)S(1)} %get-tuple-element.316), channel_id=1, source_target_pairs={{0,1},{1,2},{2,3},{4,5},{5,6},{6,7},{8,9},{9,10},{10,11},{12,13},{... | collective-permute-start | bytes 147464 | tf_op jit(solution)/shard_map/ppermute | solution.py:16
  1013.4 13.3 %collective-permute-start.9 = (bf16[1,96,256]{2,1,0:T(8,128)(2,1)S(1)}, bf16[1,96,256]{2,1,0:T(8,128)(2,1)S(1)}, u32[]{:S(2)}, u32[]{:S(2)}) collective-permute-start(bf16[1,96,256]{2,1,0:T(8,128)(2,1)S(1)} %get-tuple-element.317), channel_id=1, source_target_pairs={{4,0},{8,4},{12,8},{5,1},{9,5},{13,9},{6,2},{10,6},{14,10},{7,3},{... | collective-permute-start | bytes 147464 | tf_op jit(solution)/shard_map/ppermute | solution.py:18
  1014.7 12.0 %collective-permute-start.8 = (bf16[1,96,256]{2,1,0:T(8,128)(2,1)S(1)}, bf16[1,96,256]{2,1,0:T(8,128)(2,1)S(1)}, u32[]{:S(2)}, u32[]{:S(2)}) collective-permute-start(bf16[1,96,256]{2,1,0:T(8,128)(2,1)S(1)} %get-tuple-element.318), channel_id=1, source_target_pairs={{0,4},{4,8},{8,12},{1,5},{5,9},{9,13},{2,6},{6,10},{10,14},{3,7},{... | collective-permute-start | bytes 147464 | tf_op jit(solution)/shard_map/ppermute | solution.py:16
  1019.2 7.4 collective-permute-start.7
Sparse Core Ops, SparseCore 0:
  855.6 149.6 all-reduce.3
  1007.7 171.2 all-reduce.5
